TPU v7x, 32 devices: a whole 2x2x4 slice. The times are simulated.
32 devices in a mesh: fsdp: 8 (over z, y), ctx: 4 (over x, core).
Axes of the slice: x: 2, y: 2, z: 4, core: 2. Of those that a mesh axis runs over, the one named last changes fastest.
Arguments:
- tokens: bfloat16 [8, 1024, 2048], P('fsdp', 'ctx'), may hold values from -6 to 6
- norm_gain: bfloat16 [2048], P('fsdp'), may hold values from 0.5 to 1.5
- w_in: bfloat16 [2048, 8512], P('fsdp'), may hold values from -0.125 to 0.125
- conv_w: bfloat16 [4, 4352], P(None, 'fsdp'), may hold values from -3 to 3
- conv_b: bfloat16 [4352], P('fsdp'), may hold values from -0.5 to 0.5
- dt_bias: float32 [64], replicated, may hold values from -4.5 to -3
- a_log: float32 [64], replicated, may hold values from -7 to 0.5
- d_skip: float32 [64], replicated, may hold values from 0.5 to 2
- gate_gain: bfloat16 [4096], P('fsdp'), may hold values from 0.5 to 1.5
- w_out: bfloat16 [4096, 2048], P('fsdp'), may hold values from -0.09375 to 0.09375
- cotangent: bfloat16 [8, 1024, 2048], P('fsdp', 'ctx'), may hold values from -6 to 6
Outputs:
- output: bfloat16 [8, 1024, 2048], P('fsdp', 'ctx')
- grad_tokens: float32 [8, 1024, 2048], P('fsdp', 'ctx')
- grad_norm_gain: float32 [2048], P('fsdp')
- grad_w_in: float32 [2048, 8512], P('fsdp')
- grad_conv_w: float32 [4, 4352], P(None, 'fsdp')
- grad_conv_b: float32 [4352], P('fsdp')
- grad_dt_bias: float32 [64], replicated
- grad_a_log: float32 [64], replicated
- grad_d_skip: float32 [64], replicated
- grad_gate_gain: float32 [4096], P('fsdp')
- grad_w_out: float32 [4096, 2048], P('fsdp')
All inputs are finite; a program needn't handle non-finite values.
Results may differ from a plain program's by a relative error of at most 0.0085.
The roundings to bfloat16 on the way count: a program that leaves them out, or rounds other values in their place, can miss the bound.
Values may be sent and summed in bfloat16 or wider, within the bound.
No kernel may reach another device: no remote copies, remote signals or barrier semaphores. Data moves between devices by JAX's collectives and lax.ppermute only.
A program may use at most 320 MiB of HBM per device.

v0:
```python
import jax
import jax.numpy as jnp
from jax import lax
from jax.sharding import PartitionSpec as P

HEADS = 64
HEADDIM = 64
STATE = 128
KW = 4
GROUP = 256
CONV = 4352
EPS = 1e-05


def passed_along(block, axis, distance):
    devices = range(lax.axis_size(axis))
    route = [(i - distance, i) for i in devices if i - distance in devices]
    return lax.ppermute(block, axis, route)


def carried_in(part, axis, combine, identity, reverse):
    count = lax.axis_size(axis)
    place = lax.axis_index(axis)
    ahead = count - 1 - place if reverse else place
    gathered = jax.tree.map(lambda a: lax.all_gather(a, axis), part)
    state = jax.tree.map(lambda a, e: jnp.zeros_like(a) + jnp.asarray(e, a.dtype), part, identity)

    def one(turn, state):
        source = count - 1 - turn if reverse else turn
        return combine(
            state, jax.tree.map(lambda a: lax.dynamic_index_in_dim(a, source, 0, False), gathered)
        )

    return lax.fori_loop(0, ahead, one, state)


def in_norm(values, gain_vec):
    inverse = lax.rsqrt(jnp.mean(values * values, axis=-1, keepdims=True) + EPS)
    return values * inverse * gain_vec


def gate_norm(ssd_out, gate_z, gain_vec):
    gated = ssd_out * jax.nn.silu(gate_z)
    inverse = lax.rsqrt(jnp.mean(gated * gated, axis=-1, keepdims=True) + EPS)
    return gated * inverse * gain_vec


def conv_silu(padded, taps, offsets_bias):
    length = padded.shape[0] - taps.shape[0] + 1
    summed = offsets_bias[None, :] + taps[0][None, :] * padded[0:length]
    for offset in range(1, taps.shape[0]):
        summed = summed + taps[offset][None, :] * padded[offset : offset + length]
    return jax.nn.silu(summed)


def decay_matrix(cumulative):
    count = cumulative.shape[0]
    row_index = lax.broadcasted_iota(jnp.int32, (count, count), 0)
    col_index = lax.broadcasted_iota(jnp.int32, (count, count), 1)
    lower = (row_index >= col_index)[None]
    differ = cumulative.T[:, :, None] - cumulative.T[:, None, :]
    return jnp.where(lower, jnp.exp(jnp.where(lower, differ, 0.0)), 0.0)


def block_weighted(b_block, cumulative, step_sizes):
    tail_vals = jnp.exp(cumulative[-1][None, :] - cumulative) * step_sizes
    weighted = (tail_vals.T[:, :, None] * b_block.astype(jnp.float32)[None]).astype(jnp.bfloat16)
    return (tail_vals, weighted)


def link_states(earlier, later):
    return (earlier[0] * later[0], later[0][:, None, None] * earlier[1] + later[1])


def body(
    tokens, norm_gain, w_in, conv_w, conv_b, dt_bias, a_log, d_skip, gate_gain, w_out, cotangent
):
    gathered = (
        lax.all_gather(norm_gain, "fsdp", axis=0, tiled=True),
        lax.all_gather(w_in, "fsdp", axis=0, tiled=True),
        lax.all_gather(conv_w, "fsdp", axis=1, tiled=True),
        lax.all_gather(conv_b, "fsdp", axis=0, tiled=True),
        lax.all_gather(gate_gain, "fsdp", axis=0, tiled=True),
        lax.all_gather(w_out, "fsdp", axis=0, tiled=True),
    )
    norm_full, w_in_full, conv_w_full, conv_b_full, gate_full, w_out_full = gathered
    inputs = tokens[0].astype(jnp.float32)
    length = inputs.shape[0]
    inner_width = HEADS * HEADDIM
    blocks = length // GROUP
    normed_f, norm_back = jax.vjp(in_norm, inputs, norm_full.astype(jnp.float32))
    normed = normed_f.astype(jnp.bfloat16)
    proj = jnp.dot(normed, w_in_full, preferred_element_type=jnp.float32).astype(jnp.bfloat16)
    gate_z = proj[:, :inner_width].astype(jnp.float32)
    conv_in = proj[:, inner_width : inner_width + CONV]
    dt_raw = proj[:, inner_width + CONV :].astype(jnp.float32)
    halo_rows = passed_along(conv_in[length - KW + 1 :], "ctx", 1)
    padded = jnp.concatenate([halo_rows, conv_in], axis=0).astype(jnp.float32)
    activated, conv_back_fn = jax.vjp(
        conv_silu, padded, conv_w_full.astype(jnp.float32), conv_b_full.astype(jnp.float32)
    )
    act_low = activated.astype(jnp.bfloat16)
    x_all = act_low[:, :inner_width].reshape(blocks, GROUP, HEADS, HEADDIM)
    b_all = act_low[:, inner_width : inner_width + STATE].reshape(blocks, GROUP, STATE)
    c_all = act_low[:, inner_width + STATE :].reshape(blocks, GROUP, STATE)
    dt_in = dt_raw + dt_bias[None, :]
    step_sizes = jax.nn.softplus(dt_in)
    a_neg = -jnp.exp(a_log)
    step_all = step_sizes.reshape(blocks, GROUP, HEADS)
    piece_log = jnp.sum(step_sizes * a_neg[None, :], axis=0)
    zero_state = jnp.zeros((HEADS, HEADDIM, STATE), jnp.float32)

    def cumulate(step_block):
        return jnp.cumsum(step_block * a_neg[None, :], axis=0)

    def state_step(state, pieces):
        x_block, b_block, step_block = pieces
        cumulative = cumulate(step_block)
        tail_vals, weighted = block_weighted(b_block, cumulative, step_block)
        local = jnp.einsum("jhp,hjn->hpn", x_block, weighted, preferred_element_type=jnp.float32)
        return (jnp.exp(cumulative[-1])[:, None, None] * state + local, None)

    end_state, unused = lax.scan(state_step, zero_state, (x_all, b_all, step_all))
    identity = (jnp.ones((HEADS,), jnp.float32), zero_state)
    prefix = carried_in((jnp.exp(piece_log), end_state), "ctx", link_states, identity, False)
    start_state = prefix[1]

    def forward_step(state, pieces):
        x_block, b_block, c_block, step_block = pieces
        cumulative = cumulate(step_block)
        gram = jnp.einsum("in,jn->ij", c_block, b_block, preferred_element_type=jnp.float32)
        scores = (gram[None] * decay_matrix(cumulative) * step_block.T[:, None, :]).astype(
            jnp.bfloat16
        )
        intra = jnp.einsum("hij,jhp->ihp", scores, x_block, preferred_element_type=jnp.float32)
        inner = jnp.einsum(
            "in,hpn->ihp", c_block, state.astype(jnp.bfloat16), preferred_element_type=jnp.float32
        )
        tail_vals, weighted = block_weighted(b_block, cumulative, step_block)
        local = jnp.einsum("jhp,hjn->hpn", x_block, weighted, preferred_element_type=jnp.float32)
        new_state = jnp.exp(cumulative[-1])[:, None, None] * state + local
        return (new_state, (intra + jnp.exp(cumulative)[:, :, None] * inner, state))

    unused_end, (block_out, block_starts) = lax.scan(
        forward_step, start_state, (x_all, b_all, c_all, step_all)
    )
    xs_float = x_all.reshape(length, HEADS, HEADDIM).astype(jnp.float32)
    ssd_out = (
        block_out.reshape(length, HEADS, HEADDIM) + d_skip[None, :, None] * xs_float
    ).reshape(length, inner_width)
    mixed_f, gate_back = jax.vjp(gate_norm, ssd_out, gate_z, gate_full.astype(jnp.float32))
    mixed = mixed_f.astype(jnp.bfloat16)
    branch = jnp.dot(mixed, w_out_full, preferred_element_type=jnp.float32)
    output = (inputs + branch).astype(jnp.bfloat16)[None]
    regathered = (
        lax.all_gather(norm_gain, "fsdp", axis=0, tiled=True),
        lax.all_gather(w_in, "fsdp", axis=0, tiled=True),
        lax.all_gather(conv_w, "fsdp", axis=1, tiled=True),
        lax.all_gather(conv_b, "fsdp", axis=0, tiled=True),
        lax.all_gather(gate_gain, "fsdp", axis=0, tiled=True),
        lax.all_gather(w_out, "fsdp", axis=0, tiled=True),
    )
    w_in_full = regathered[1]
    w_out_full = regathered[5]
    seed = cotangent[0]
    d_w_out = jnp.einsum("td,te->de", mixed, seed, preferred_element_type=jnp.float32)
    d_mixed = jnp.einsum("te,de->td", seed, w_out_full, preferred_element_type=jnp.float32)
    d_ssd_f, d_gate_z, d_gate_gain = gate_back(d_mixed)
    d_ssd = d_ssd_f.astype(jnp.bfloat16)
    d_ssd3 = d_ssd.astype(jnp.float32).reshape(length, HEADS, HEADDIM)
    d_skip_grad = jnp.sum(d_ssd3 * xs_float, axis=(0, 2))
    d_all = d_ssd.reshape(blocks, GROUP, HEADS, HEADDIM)

    def grad_state_step(carried, pieces):
        c_block, step_block, d_block = pieces
        cumulative = cumulate(step_block)
        d_inner = (d_block.astype(jnp.float32) * jnp.exp(cumulative)[:, :, None]).astype(
            jnp.bfloat16
        )
        from_out = jnp.einsum("ihp,in->hpn", d_inner, c_block, preferred_element_type=jnp.float32)
        return (jnp.exp(cumulative[-1])[:, None, None] * carried + from_out, None)

    grad_local, unused = lax.scan(
        grad_state_step, zero_state, (c_all, step_all, d_all), reverse=True
    )
    identity_back = (jnp.ones((HEADS,), jnp.float32), zero_state)
    suffix = carried_in((jnp.exp(piece_log), grad_local), "ctx", link_states, identity_back, True)
    end_grad = suffix[1]

    def grad_step(carried, pieces):
        x_block, b_block, c_block, step_block, d_block, state = pieces
        b_float = b_block.astype(jnp.float32)
        d_float = d_block.astype(jnp.float32)
        cumulative = cumulate(step_block)
        last_decay = jnp.exp(cumulative[-1])
        tail_vals, weighted = block_weighted(b_block, cumulative, step_block)
        d_state = last_decay[:, None, None] * carried
        d_last = jnp.sum(carried * state, axis=(1, 2)) * last_decay
        d_local = carried.astype(jnp.bfloat16)
        d_x = jnp.einsum("hjn,hpn->jhp", weighted, d_local, preferred_element_type=jnp.float32)
        d_weighted = jnp.einsum(
            "jhp,hpn->hjn", x_block, d_local, preferred_element_type=jnp.float32
        )
        d_b = jnp.sum(d_weighted * tail_vals.T[:, :, None], axis=0)
        d_tail = jnp.sum(d_weighted * b_float[None], axis=2).T
        d_step = d_tail * jnp.exp(cumulative[-1][None, :] - cumulative)
        tail_log = d_tail * tail_vals
        d_last = d_last + jnp.sum(tail_log, axis=0)
        d_cum = -tail_log
        growth = jnp.exp(cumulative)
        state_low = state.astype(jnp.bfloat16)
        inner = jnp.einsum("in,hpn->ihp", c_block, state_low, preferred_element_type=jnp.float32)
        d_cum = d_cum + jnp.sum(d_float * inner, axis=2) * growth
        d_inner = (d_float * growth[:, :, None]).astype(jnp.bfloat16)
        d_c = jnp.einsum("ihp,hpn->in", d_inner, state_low, preferred_element_type=jnp.float32)
        d_state = d_state + jnp.einsum(
            "ihp,in->hpn", d_inner, c_block, preferred_element_type=jnp.float32
        )
        gram = jnp.einsum("in,jn->ij", c_block, b_block, preferred_element_type=jnp.float32)
        decays = decay_matrix(cumulative)
        step_cols = step_block.T[:, None, :]
        scores = (gram[None] * decays * step_cols).astype(jnp.bfloat16)
        d_scores = jnp.einsum("ihp,jhp->hij", d_block, x_block, preferred_element_type=jnp.float32)
        d_x = d_x + jnp.einsum("hij,ihp->jhp", scores, d_block, preferred_element_type=jnp.float32)
        common = d_scores * decays
        d_gram = jnp.sum(common * step_cols, axis=0).astype(jnp.bfloat16)
        d_step = d_step + jnp.sum(common * gram[None], axis=1).T
        exponent = common * gram[None] * step_cols
        d_cum = d_cum + jnp.sum(exponent, axis=2).T - jnp.sum(exponent, axis=1).T
        d_c = d_c + jnp.einsum("ij,jn->in", d_gram, b_block, preferred_element_type=jnp.float32)
        d_b = d_b + jnp.einsum("ij,in->jn", d_gram, c_block, preferred_element_type=jnp.float32)
        last_row = lax.broadcasted_iota(jnp.int32, d_cum.shape, 0) == d_cum.shape[0] - 1
        d_cum = d_cum + jnp.where(last_row, d_last[None, :], 0.0)
        d_rate = jnp.cumsum(d_cum[::-1], axis=0)[::-1]
        return (d_state, (d_x, d_b, d_c, d_step, d_rate))

    unused_grad, block_grads = lax.scan(
        grad_step, end_grad, (x_all, b_all, c_all, step_all, d_all, block_starts), reverse=True
    )
    d_x_all, d_b_all, d_c_all, d_step_all, d_rate_all = block_grads
    d_rate_flat = d_rate_all.reshape(length, HEADS)
    d_x_flat = (d_x_all.reshape(length, HEADS, HEADDIM) + d_skip[None, :, None] * d_ssd3).reshape(
        length, inner_width
    )
    d_act = jnp.concatenate(
        [d_x_flat, d_b_all.reshape(length, STATE), d_c_all.reshape(length, STATE)], axis=1
    )
    d_padded, d_conv_w, d_conv_b = conv_back_fn(d_act)
    returned = passed_along(d_padded[: KW - 1].astype(jnp.bfloat16), "ctx", -1).astype(jnp.float32)
    d_conv_in = d_padded[KW - 1 :] + jnp.concatenate(
        [jnp.zeros((length - KW + 1, CONV), jnp.float32), returned], axis=0
    )
    d_step_total = d_step_all.reshape(length, HEADS) + d_rate_flat * a_neg[None, :]
    d_dt_in = d_step_total * jax.nn.sigmoid(dt_in)
    d_dt_bias = jnp.sum(d_dt_in, axis=0)
    d_a_log = jnp.sum(d_rate_flat * step_sizes, axis=0) * a_neg
    d_proj = jnp.concatenate([d_gate_z, d_conv_in, d_dt_in], axis=1).astype(jnp.bfloat16)
    d_w_in = jnp.einsum("td,tk->dk", normed, d_proj, preferred_element_type=jnp.float32)
    d_normed = jnp.einsum("tk,dk->td", d_proj, w_in_full, preferred_element_type=jnp.float32)
    d_inputs, d_norm_gain = norm_back(d_normed)
    grad_tokens = (seed.astype(jnp.float32) + d_inputs)[None]
    shares = (
        lax.psum_scatter(d_norm_gain, "fsdp", scatter_dimension=0, tiled=True),
        lax.psum_scatter(d_w_in, "fsdp", scatter_dimension=0, tiled=True),
        lax.psum_scatter(d_conv_w, "fsdp", scatter_dimension=1, tiled=True),
        lax.psum_scatter(d_conv_b, "fsdp", scatter_dimension=0, tiled=True),
        lax.psum_scatter(d_gate_gain, "fsdp", scatter_dimension=0, tiled=True),
        lax.psum_scatter(d_w_out, "fsdp", scatter_dimension=0, tiled=True),
    )
    summed = lax.psum((shares[0], shares[1], shares[2], shares[3], shares[4], shares[5]), "ctx")
    head_sums = lax.psum((d_dt_bias, d_a_log, d_skip_grad), ("fsdp", "ctx"))
    return (
        output,
        grad_tokens,
        summed[0],
        summed[1],
        summed[2],
        summed[3],
        head_sums[0],
        head_sums[1],
        head_sums[2],
        summed[4],
        summed[5],
    )


def solution(mesh):
    in_specs = (
        P("fsdp", "ctx", None),
        P("fsdp"),
        P("fsdp", None),
        P(None, "fsdp"),
        P("fsdp"),
        P(),
        P(),
        P(),
        P("fsdp"),
        P("fsdp", None),
        P("fsdp", "ctx", None),
    )
    out_specs = (
        P("fsdp", "ctx", None),
        P("fsdp", "ctx", None),
        P("fsdp"),
        P("fsdp", None),
        P(None, "fsdp"),
        P("fsdp"),
        P(),
        P(),
        P(),
        P("fsdp"),
        P("fsdp", None),
    )
    return jax.shard_map(body, mesh=mesh, in_specs=in_specs, out_specs=out_specs, check_vma=False)
```

profile of v0, /device:TPU:0, one launch (start us, length us, event | category | flops | bytes accessed | tf_op | source)
XLA Modules:
  0.0 3068.2 jit_solution(707199861307095639)
XLA Ops:
  8.1 63.6 %all-gather.4 = bf16[8,1,256]{2,1,0:T(2,128)(2,1)S(1)} all-gather(bf16[1,1,256]{2,1,0:T(2,128)(2,1)S(1)} %reshape.249), channel_id=1, replica_groups=mesh['fsdp'=8,'ctx'=4] {'fsdp'}, dimensions={0}, use_global_device_ids=true | all-gather | bytes 4608 | tf_op jit(solution)/shard_map/all_gather | solution.py:79
  71.7 30.6 all-gather.3
  104.0 75.0 %all-reduce.9 = bf16[4352]{0:T(1024)(128)(2,1)S(1)} all-reduce(bf16[4352]{0:T(1024)(128)(2,1)S(1)} %dynamic-update-slice), channel_id=1, replica_groups=mesh['fsdp'=8,'ctx'=4] {'fsdp'}, use_global_device_ids=true, to_apply=%add.9 | all-reduce | flops 4352 | bytes 17408
  179.6 498.4 %all-gather.11.cloned.1.call-done = bf16[2048,8512]{0,1:T(8,128)(2,1)} async-done(((bf16[256,8512]{0,1:T(8,128)(2,1)}), bf16[2048,8512]{0,1:T(8,128)(2,1)}) %all-gather.11.cloned.1.call-update) | async-done | bytes 34865168 | tf_op jit(solution)/shard_map/all_gather | solution.py:80
  678.0 17.2 convolution_convert_fusion
  718.4 26.6 all-gather.5
  752.5 23.1 all-gather.15.cloned.1.call-done
  797.8 207.6 %all-gather.13.cloned.1.call-done = bf16[4096,2048]{1,0:T(8,128)(2,1)} async-done(((bf16[512,2048]{1,0:T(8,128)(2,1)}), bf16[4096,2048]{1,0:T(8,128)(2,1)}) %all-gather.13.cloned.1.call-update) | async-done | bytes 16777232 | tf_op jit(solution)/shard_map/all_gather | solution.py:84
  1005.4 20.1 multiply_reduce_fusion.10
  1026.2 9.7 fusion.12
  1043.9 17.6 fusion.48
  1062.5 12.5 multiply_reduce_fusion.2
  1082.9 7.7 fusion.1
  1090.6 9.7 all-gather.17.cloned.1.call-done
  1101.8 13.9 while.17
  1162.6 26.9 fusion.39
  1192.0 455.4 %reduce-scatter.8.cloned.1.call-done = f32[512,2048]{1,0:T(8,128)} async-done(((f32[4096,2048]{1,0:T(8,128)}), f32[512,2048]{1,0:T(8,128)}) %reduce-scatter.8.cloned.1.call-update) | async-done | bytes 4194320 | tf_op jit(solution)/shard_map/reduce_scatter | solution.py:268
  1647.4 1103.3 %reduce-scatter.6.cloned.1.call-done = f32[256,8512]{0,1:T(8,128)} async-done(((f32[2048,8512]{0,1:T(8,128)}), f32[256,8512]{0,1:T(8,128)}) %reduce-scatter.6.cloned.1.call-update) | async-done | bytes 8716304 | tf_op jit(solution)/shard_map/reduce_scatter | solution.py:264
  2753.0 12.6 fusion.27
  2765.6 39.7 %all-reduce.14 = (f32[64]{0:T(128)}, f32[64]{0:T(128)}, f32[64]{0:T(128)}) all-reduce(f32[64]{0:T(128)S(1)} %get-tuple-element.299, f32[64]{0:T(128)S(1)} %fusion.83, f32[64]{0:T(128)S(1)} %reduce_sum.298), channel_id=1, replica_groups=mesh['fsdp'=8,'ctx'=4] {'fsdp','ctx'}, use_global_device_ids=true, to_apply=%region_37.38 | all-reduce | flops 192 | bytes 1536 | tf_op jit(solution)/shard_map/psum | solution.py:271
  2805.2 17.6 fusion.30
  2822.9 37.4 %all-reduce.15 = (f32[2048]{0:T(1024)S(1)}, f32[4352]{0:T(1024)S(1)}, f32[4096]{0:T(1024)S(1)}) all-reduce(f32[2048]{0:T(1024)S(1)} %get-tuple-element.259, f32[4352]{0:T(1024)S(1)} %get-tuple-element.258, f32[4096]{0:T(1024)S(1)} %copy-done.39), channel_id=5, replica_groups=mesh['fsdp'=8,'ctx'=4] {'fsdp'}, use_global_device_ids=true, to_apply=%region_23.24.clone | all-reduce | flops 10496 | bytes 83968
  2865.6 12.8 all-reduce.16
  2878.4 173.4 %all-reduce.20.cloned.1.call-done = (f32[256,8512]{0,1:T(8,128)}, f32[512,2048]{1,0:T(8,128)}) async-done(((f32[256,8512]{0,1:T(8,128)}, f32[512,2048]{1,0:T(8,128)}), (f32[256,8512]{0,1:T(8,128)}, f32[512,2048]{1,0:T(8,128)})) %all-reduce.20.cloned.1.call-update) | async-done | bytes 12910608 | tf_op jit(solution)/shard_map/psum | solution.py:270
  (264 shorter events, 150.5 us)
Async XLA Ops:
  7.2 95.2 %copy-start.46 = (u32[32]{0:T(128)S(1)}, u32[32]{0:T(128)}, u32[]{:S(2)}) copy-start(u32[32]{0:T(128)} %constant.172) | copy-start | bytes 388
  7.2 64.4 %copy-start.43 = (bf16[4,544]{1,0:T(4,128)(2,1)S(1)}, bf16[4,544]{1,0:T(4,128)(2,1)}, u32[]{:S(2)}) copy-start(bf16[4,544]{1,0:T(4,128)(2,1)} %param.18) | copy-start | bytes 13060
  7.2 96.5 %copy-start.48 = (bf16[544]{0:T(1024)(128)(2,1)S(1)}, bf16[544]{0:T(1024)(128)(2,1)}, u32[]{:S(2)}) copy-start(bf16[544]{0:T(1024)(128)(2,1)} %param.19) | copy-start | bytes 3268
  7.2 172.0 %copy-start.5 = (bf16[1,256,2048]{2,1,0:T(8,128)(2,1)S(1)}, bf16[1,256,2048]{2,1,0:T(8,128)(2,1)}, u32[]{:S(2)}) copy-start(bf16[1,256,2048]{2,1,0:T(8,128)(2,1)} %param.15) | copy-start | bytes 3145732
  7.2 172.3 %copy-start.58 = (f32[64]{0:T(128)S(1)}, f32[64]{0:T(128)}, u32[]{:S(2)}) copy-start(f32[64]{0:T(128)} %param.21) | copy-start | bytes 772
  7.2 670.7 %all-gather.11.cloned.1.call-start = ((), (), s32[]{:S(2)}) async-start(), calls=%async_computation.3 | async-start | bytes 39223296 | tf_op jit(solution)/shard_map/all_gather | solution.py:80
  8.0 767.6 %all-gather.15.cloned.1.call-start = ((), (), s32[]{:S(2)}) async-start(), calls=%async_computation.7 | async-start | bytes 10485760 | tf_op jit(solution)/shard_map/all_gather | solution.py:25
  71.6 606.3 %copy-start.10 = (f32[8,1,256]{2,1,0:T(1,128)}, f32[8,1,256]{2,1,0:T(1,128)S(1)}, u32[]{:S(2)}) copy-start(f32[8,1,256]{2,1,0:T(1,128)S(1)} %convert_element_type.136) | copy-start | bytes 24580
  179.2 522.2 %copy-start.21 = (f32[4352]{0:T(1024)}, f32[4352]{0:T(1024)S(1)}, u32[]{:S(2)}) copy-start(f32[4352]{0:T(1024)S(1)} %get-tuple-element.261) | copy-start | bytes 52228
  179.2 522.2 %copy-start.23 = (f32[4352]{0:T(1024)}, f32[4352]{0:T(1024)S(1)}, u32[]{:S(2)}) copy-start(f32[4352]{0:T(1024)S(1)} %get-tuple-element.262) | copy-start | bytes 52228
  179.2 522.2 %copy-start.25 = (f32[4352]{0:T(1024)}, f32[4352]{0:T(1024)S(1)}, u32[]{:S(2)}) copy-start(f32[4352]{0:T(1024)S(1)} %get-tuple-element.263) | copy-start | bytes 52228
  179.2 522.2 %copy-start.27 = (f32[4352]{0:T(1024)}, f32[4352]{0:T(1024)S(1)}, u32[]{:S(2)}) copy-start(f32[4352]{0:T(1024)S(1)} %get-tuple-element.264) | copy-start | bytes 52228
  179.5 498.4 %copy-start.40 = (f32[256]{0:T(256)}, f32[256]{0:T(256)S(1)}, u32[]{:S(2)}) copy-start(f32[256]{0:T(256)S(1)} %fusion.33) | copy-start | bytes 3076
  179.6 518.1 %copy-start.49 = (f32[64]{0:T(128)}, f32[64]{0:T(128)S(1)}, u32[]{:S(2)}) copy-start(f32[64]{0:T(128)S(1)} %exponential_negate_fusion) | copy-start | bytes 772
  179.6 498.4 %copy-start.12 = (f32[256]{0:T(256)}, f32[256]{0:T(256)S(1)}, u32[]{:S(2)}) copy-start(f32[256]{0:T(256)S(1)} %fusion.76) | copy-start | bytes 3076
  696.2 4.7 collective-permute-start
  716.2 289.2 %all-gather.13.cloned.1.call-start = ((), (), s32[]{:S(2)}) async-start(), calls=%async_computation.4 | async-start | bytes 18874368 | tf_op jit(solution)/shard_map/all_gather | solution.py:84
  717.0 383.3 %all-gather.17.cloned.1.call-start = ((), (), s32[]{:S(2)}) async-start(), calls=%async_computation.8 | async-start | bytes 10485760 | tf_op jit(solution)/shard_map/all_gather | solution.py:25
  790.7 214.7 %copy-start.8 = (bf16[1,256,2048]{2,1,0:T(8,128)(2,1)S(1)}, bf16[1,256,2048]{2,1,0:T(8,128)(2,1)}, u32[]{:S(2)}) copy-start(bf16[1,256,2048]{2,1,0:T(8,128)(2,1)} %param.25) | copy-start | bytes 3145732
  1043.7 603.7 %reduce-scatter.8.cloned.1.call-start = ((), (), s32[]{:S(2)}) async-start(), calls=%async_computation.6 | async-start | bytes 37748736 | tf_op jit(solution)/shard_map/reduce_scatter | solution.py:268
  1061.6 1689.1 %reduce-scatter.6.cloned.1.call-start = ((), (), s32[]{:S(2)}) async-start(), calls=%async_computation.5 | async-start | bytes 78446592 | tf_op jit(solution)/shard_map/reduce_scatter | solution.py:264
  1158.9 3.2 collective-permute-start.1
  1189.5 1675.0 %reduce-scatter.10.cloned.1.call-start = ((), (), s32[]{:S(2)}) async-start(), calls=%async_computation.9 | async-start | bytes 2506752
  1191.9 1859.8 %all-reduce.20.cloned.1.call-start = ((), (), s32[]{:S(2)}) async-start(), calls=%async_computation.10 | async-start | bytes 25821184 | tf_op jit(solution)/shard_map/psum | solution.py:270
  (50 other events, 484.7 us)
Sparse Core Ops, SparseCore 0:
  9.5 668.3 all-gather.10
  716.3 59.2 all-gather.14
  777.7 227.6 all-gather.12
  1043.8 56.4 all-gather.16
  1103.9 543.4 reduce-scatter.7
  1651.1 1099.4 reduce-scatter.5
  2755.1 67.8 reduce-scatter.9
  2825.9 225.8 all-reduce.19
where the time goes:
time: 3080 us; the launch traced here: 3070 us
  waiting for transfers between devices  2470 us (80%)
  blocking collectives  292 us (9%)
  matrix products  164 us (5%)
  other arithmetic  70 us (2%)
  local copies, waits for them, and re-layouts  46.4 us (2%)
    reduce_scatter x1, waiting for transfers between devices, body(): lax.psum_scatter(d_w_in, 'fsdp', scatter_dimension=0, tiled=True)  1100 us
    all_gather x1, waiting for transfers between devices, body(): lax.all_gather(w_in, 'fsdp', axis=0, tiled=True)  498 us
    reduce_scatter x1, waiting for transfers between devices, body(): lax.psum_scatter(d_w_out, 'fsdp', scatter_dimension=0, tiled=True)  455 us
    all_gather x1, waiting for transfers between devices, body(): lax.all_gather(w_out, 'fsdp', axis=0, tiled=True)  208 us
    psum x1, waiting for transfers between devices, body(): lax.psum((shares[0], shares[1], shares[2], shares[3], shares[4], shares[5...  173 us
    unnamed x3, blocking collectives  119 us
    all_gather x1, blocking collectives, body(): lax.all_gather(norm_gain, 'fsdp', axis=0, tiled=True)  63.6 us
  transfers between devices with their start and end apart: 10, of which 8 were waited for; matrix products, arithmetic and copies ran while one was open for 6% of the time, Pallas kernels for 0%

commit v1 on v0

--- a/solution.py
+++ b/solution.py
@@ -12,6 +12,22 @@
 EPS = 1e-05
 
 
+def ring_gather(x, axis, dim):
+    ways, here, lap = (lax.axis_size(axis), lax.axis_index(axis), x.shape[dim])
+    dims = [n * ways if d == dim else n for d, n in enumerate(x.shape)]
+    full = lax.dynamic_update_slice_in_dim(jnp.zeros(dims, x.dtype), x, here * lap, axis=dim)
+    going_up = going_down = x
+    for far in range(1, ways // 2 + 1):
+        going_up = lax.ppermute(going_up, axis, [(d, (d + 1) % ways) for d in range(ways)])
+        full = lax.dynamic_update_slice_in_dim(full, going_up, (here - far) % ways * lap, axis=dim)
+        if 2 * far < ways:
+            going_down = lax.ppermute(going_down, axis, [(d, (d - 1) % ways) for d in range(ways)])
+            full = lax.dynamic_update_slice_in_dim(
+                full, going_down, (here + far) % ways * lap, axis=dim
+            )
+    return full
+
+
 def passed_along(block, axis, distance):
     devices = range(lax.axis_size(axis))
     route = [(i - distance, i) for i in devices if i - distance in devices]
@@ -77,7 +93,7 @@
 ):
     gathered = (
         lax.all_gather(norm_gain, "fsdp", axis=0, tiled=True),
-        lax.all_gather(w_in, "fsdp", axis=0, tiled=True),
+        ring_gather(w_in, "fsdp", 0),
         lax.all_gather(conv_w, "fsdp", axis=1, tiled=True),
         lax.all_gather(conv_b, "fsdp", axis=0, tiled=True),
         lax.all_gather(gate_gain, "fsdp", axis=0, tiled=True),

time: 3080 us -> 3810 us (1.24)
  waiting for transfers between devices: 2470 us -> 2990 us
  blocking collectives: 292 us -> 457 us
  local copies, waits for them, and re-layouts: 46.4 us -> 86.1 us
    ppermute x0 -> x7, waiting for transfers between devices: none -> 350 us  [the longest x4 184 us: ring_gather(): lax.ppermute(going_up, axis, [(d, (d + 1) % ways) for d in range(ways)])]
    all_gather x1, waiting for transfers between devices: 498 us -> 663 us  [body(): lax.all_gather(w_in, 'fsdp', axis=0, tiled=True)]
    all_gather x1, blocking collectives: 63.6 us -> 197 us  [body(): lax.all_gather(norm_gain, 'fsdp', axis=0, tiled=True)]
  transfers between devices with their start and end apart: 10 -> 17, of which waited for: 8 -> 11; matrix products, arithmetic and copies ran while one was open for 6% -> 6% of each run, Pallas kernels for 0% -> 0%
where the time goes in v1:
time: 3810 us
  waiting for transfers between devices  2990 us (78%)
  blocking collectives  457 us (12%)
  matrix products  165 us (4%)
  local copies, waits for them, and re-layouts  86.1 us (2%)
  other arithmetic  71.9 us (2%)
    reduce_scatter x1, waiting for transfers between devices, body(): lax.psum_scatter(d_w_in, 'fsdp', scatter_dimension=0, tiled=True)  1100 us
    all_gather x1, waiting for transfers between devices, body(): lax.all_gather(w_in, 'fsdp', axis=0, tiled=True)  663 us
    reduce_scatter x1, waiting for transfers between devices, body(): lax.psum_scatter(d_w_out, 'fsdp', scatter_dimension=0, tiled=True)  454 us
    all_gather x1, waiting for transfers between devices, body(): lax.all_gather(w_out, 'fsdp', axis=0, tiled=True)  208 us
    all_gather x1, blocking collectives, body(): lax.all_gather(norm_gain, 'fsdp', axis=0, tiled=True)  197 us
    ppermute x4, waiting for transfers between devices, ring_gather(): lax.ppermute(going_up, axis, [(d, (d + 1) % ways) for d in range(ways)])  184 us
    ppermute x3, waiting for transfers between devices, ring_gather(): lax.ppermute(going_down, axis, [(d, (d - 1) % ways) for d in range(ways)])  166 us
    psum x1, waiting for transfers between devices, body(): lax.psum((shares[0], shares[1], shares[2], shares[3], shares[4], shares[5...  160 us
  transfers between devices with their start and end apart: 17, of which 11 were waited for; matrix products, arithmetic and copies ran while one was open for 6% of the time, Pallas kernels for 0%

profile of v1, /device:TPU:0, one launch (start us, length us, event | category | flops | bytes accessed | tf_op | source)
XLA Modules:
  0.0 3805.1 jit_solution(12126986416169650047)
XLA Ops:
  13.3 183.9 %collective-permute-done = bf16[256,8512]{0,1:T(8,128)(2,1)} collective-permute-done((bf16[256,8512]{0,1:T(8,128)(2,1)}, bf16[256,8512]{0,1:T(8,128)(2,1)}, u32[]{:S(2)}, u32[]{:S(2)}) %collective-permute-start) | collective-permute-done | bytes 4358176 | tf_op jit(solution)/shard_map/ppermute | solution.py:21
  203.5 197.4 %all-gather.4 = bf16[8,1,256]{2,1,0:T(2,128)(2,1)S(1)} all-gather(bf16[1,1,256]{2,1,0:T(2,128)(2,1)S(1)} %reshape.249), channel_id=1, replica_groups=mesh['fsdp'=8,'ctx'=4] {'fsdp'}, dimensions={0}, use_global_device_ids=true | all-gather | bytes 4608 | tf_op jit(solution)/shard_map/all_gather | solution.py:95
  400.9 30.9 all-gather.3
  434.9 110.1 %all-reduce.9 = bf16[4352]{0:T(1024)(128)(2,1)S(1)} all-reduce(bf16[4352]{0:T(1024)(128)(2,1)S(1)} %dynamic-update-slice), channel_id=1, replica_groups=mesh['fsdp'=8,'ctx'=4] {'fsdp'}, use_global_device_ids=true, to_apply=%add.9 | all-reduce | flops 4352 | bytes 17408
  582.9 165.7 %collective-permute-done.5 = bf16[256,8512]{0,1:T(8,128)(2,1)S(1)} collective-permute-done((bf16[256,8512]{0,1:T(8,128)(2,1)}, bf16[256,8512]{0,1:T(8,128)(2,1)S(1)}, u32[]{:S(2)}, u32[]{:S(2)}) %collective-permute-start.5) | collective-permute-done | bytes 4358176 | tf_op jit(solution)/shard_map/ppermute | solution.py:24
  753.1 17.3 convolution_convert_fusion
  793.5 26.0 all-gather.5
  827.2 21.1 all-gather.15.cloned.1.call-done
  870.2 207.8 %all-gather.11.cloned.1.call-done = bf16[4096,2048]{1,0:T(8,128)(2,1)} async-done(((bf16[512,2048]{1,0:T(8,128)(2,1)}), bf16[4096,2048]{1,0:T(8,128)(2,1)}) %all-gather.11.cloned.1.call-update) | async-done | bytes 16777232 | tf_op jit(solution)/shard_map/all_gather | solution.py:100
  1078.0 20.1 multiply_reduce_fusion.10
  1116.6 17.6 fusion.48
  1135.2 12.5 multiply_reduce_fusion.2
  1174.5 13.9 while.17
  1235.2 26.9 fusion.39
  1265.4 454.4 %reduce-scatter.8.cloned.1.call-done = f32[512,2048]{1,0:T(8,128)} async-done(((f32[4096,2048]{1,0:T(8,128)}), f32[512,2048]{1,0:T(8,128)}) %reduce-scatter.8.cloned.1.call-update) | async-done | bytes 4194320 | tf_op jit(solution)/shard_map/reduce_scatter | solution.py:284
  1719.8 1102.7 %reduce-scatter.6.cloned.1.call-done = f32[256,8512]{0,1:T(8,128)} async-done(((f32[2048,8512]{0,1:T(8,128)}), f32[256,8512]{0,1:T(8,128)}) %reduce-scatter.6.cloned.1.call-update) | async-done | bytes 8716304 | tf_op jit(solution)/shard_map/reduce_scatter | solution.py:280
  2824.8 12.6 fusion.27
  2837.4 39.6 %all-reduce.14 = (f32[64]{0:T(128)}, f32[64]{0:T(128)}, f32[64]{0:T(128)}) all-reduce(f32[64]{0:T(128)S(1)} %get-tuple-element.299, f32[64]{0:T(128)S(1)} %fusion.83, f32[64]{0:T(128)S(1)} %reduce_sum.298), channel_id=1, replica_groups=mesh['fsdp'=8,'ctx'=4] {'fsdp','ctx'}, use_global_device_ids=true, to_apply=%region_37.38 | all-reduce | flops 192 | bytes 1536 | tf_op jit(solution)/shard_map/psum | solution.py:287
  2877.0 17.6 reduce-scatter.10.cloned.1.call-done
  2895.7 663.2 %all-gather.13.cloned.1.call-done = bf16[2048,8512]{0,1:T(8,128)(2,1)} async-done(((bf16[256,8512]{0,1:T(8,128)(2,1)}), bf16[2048,8512]{0,1:T(8,128)(2,1)}) %all-gather.13.cloned.1.call-update) | async-done | bytes 34865168 | tf_op jit(solution)/shard_map/all_gather | solution.py:173
  3558.9 18.9 fusion.30
  3577.8 34.5 all-reduce.15
  3612.6 12.5 all-reduce.16
  3628.9 159.7 %all-reduce.20.cloned.1.call-done = (f32[256,8512]{0,1:T(8,128)}, f32[512,2048]{1,0:T(8,128)}) async-done(((f32[256,8512]{0,1:T(8,128)}, f32[512,2048]{1,0:T(8,128)}), (f32[256,8512]{0,1:T(8,128)}, f32[512,2048]{1,0:T(8,128)})) %all-reduce.20.cloned.1.call-update) | async-done | bytes 12910608 | tf_op jit(solution)/shard_map/psum | solution.py:286
  (282 shorter events, 232.7 us)
Async XLA Ops:
  7.2 841.1 %all-gather.15.cloned.1.call-start = ((), (), s32[]{:S(2)}) async-start(), calls=%async_computation.7 | async-start | bytes 10485760 | tf_op jit(solution)/shard_map/all_gather | solution.py:41
  7.2 190.1 %collective-permute-start = (bf16[256,8512]{0,1:T(8,128)(2,1)}, bf16[256,8512]{0,1:T(8,128)(2,1)}, u32[]{:S(2)}, u32[]{:S(2)}) collective-permute-start(bf16[256,8512]{0,1:T(8,128)(2,1)} %param.17), channel_id=1, source_target_pairs={{0,4},{4,8},{8,12},{12,16},{16,20},{20,24},{24,28},{28,0},{1,5},{5... | collective-permute-start | bytes 13074440 | tf_op jit(solution)/shard_map/ppermute | solution.py:21
  10.2 189.5 %collective-permute-start.1 = (bf16[256,8512]{0,1:T(8,128)(2,1)}, bf16[256,8512]{0,1:T(8,128)(2,1)}, u32[]{:S(2)}, u32[]{:S(2)}) collective-permute-start(bf16[256,8512]{0,1:T(8,128)(2,1)} %param.17), channel_id=1, source_target_pairs={{0,28},{4,0},{8,4},{12,8},{16,12},{20,16},{24,20},{28,24},{1,29},{... | collective-permute-start | bytes 13074440 | tf_op jit(solution)/shard_map/ppermute | solution.py:24
  197.3 234.5 %collective-permute-start.2 = (bf16[256,8512]{0,1:T(8,128)(2,1)}, bf16[256,8512]{0,1:T(8,128)(2,1)}, u32[]{:S(2)}, u32[]{:S(2)}) collective-permute-start(bf16[256,8512]{0,1:T(8,128)(2,1)} %collective-permute-done), channel_id=1, source_target_pairs={{0,4},{4,8},{8,12},{12,16},{16,20},{20,24},{24,28},{28,0},{1,5},{5... | collective-permute-start | bytes 13074440 | tf_op jit(solution)/shard_map/ppermute | solution.py:21
  199.8 365.6 %collective-permute-start.3 = (bf16[256,8512]{0,1:T(8,128)(2,1)}, bf16[256,8512]{0,1:T(8,128)(2,1)}, u32[]{:S(2)}, u32[]{:S(2)}) collective-permute-start(bf16[256,8512]{0,1:T(8,128)(2,1)} %collective-permute-done.1), channel_id=1, source_target_pairs={{0,28},{4,0},{8,4},{12,8},{16,12},{20,16},{24,20},{28,24},{1,29},{... | collective-permute-start | bytes 13074440 | tf_op jit(solution)/shard_map/ppermute | solution.py:24
  400.9 352.2 %copy-start.10 = (f32[8,1,256]{2,1,0:T(1,128)}, f32[8,1,256]{2,1,0:T(1,128)S(1)}, u32[]{:S(2)}) copy-start(f32[8,1,256]{2,1,0:T(1,128)S(1)} %convert_element_type.136) | copy-start | bytes 24580
  431.8 137.4 %collective-permute-start.4 = (bf16[256,8512]{0,1:T(8,128)(2,1)}, bf16[256,8512]{0,1:T(8,128)(2,1)}, u32[]{:S(2)}, u32[]{:S(2)}) collective-permute-start(bf16[256,8512]{0,1:T(8,128)(2,1)} %collective-permute-done.2), channel_id=1, source_target_pairs={{0,4},{4,8},{8,12},{12,16},{16,20},{20,24},{24,28},{28,0},{1,5},{5... | collective-permute-start | bytes 13074440 | tf_op jit(solution)/shard_map/ppermute | solution.py:21
  545.2 231.2 %copy-start.21 = (f32[4352]{0:T(1024)}, f32[4352]{0:T(1024)S(1)}, u32[]{:S(2)}) copy-start(f32[4352]{0:T(1024)S(1)} %get-tuple-element.261) | copy-start | bytes 52228
  545.3 231.2 %copy-start.23 = (f32[4352]{0:T(1024)}, f32[4352]{0:T(1024)S(1)}, u32[]{:S(2)}) copy-start(f32[4352]{0:T(1024)S(1)} %get-tuple-element.262) | copy-start | bytes 52228
  545.3 231.2 %copy-start.25 = (f32[4352]{0:T(1024)}, f32[4352]{0:T(1024)S(1)}, u32[]{:S(2)}) copy-start(f32[4352]{0:T(1024)S(1)} %get-tuple-element.263) | copy-start | bytes 52228
  545.3 231.2 %copy-start.27 = (f32[4352]{0:T(1024)}, f32[4352]{0:T(1024)S(1)}, u32[]{:S(2)}) copy-start(f32[4352]{0:T(1024)S(1)} %get-tuple-element.264) | copy-start | bytes 52228
  565.4 183.2 %collective-permute-start.5 = (bf16[256,8512]{0,1:T(8,128)(2,1)}, bf16[256,8512]{0,1:T(8,128)(2,1)S(1)}, u32[]{:S(2)}, u32[]{:S(2)}) collective-permute-start(bf16[256,8512]{0,1:T(8,128)(2,1)} %collective-permute-done.3), channel_id=1, source_target_pairs={{0,28},{4,0},{8,4},{12,8},{16,12},{20,16},{24,20},{28,24},{1,29},{... | collective-permute-start | bytes 13074440 | tf_op jit(solution)/shard_map/ppermute | solution.py:24
  569.3 181.5 %collective-permute-start.6 = (bf16[256,8512]{0,1:T(8,128)(2,1)}, bf16[256,8512]{0,1:T(8,128)(2,1)S(1)}, u32[]{:S(2)}, u32[]{:S(2)}) collective-permute-start(bf16[256,8512]{0,1:T(8,128)(2,1)} %collective-permute-done.4), channel_id=1, source_target_pairs={{0,4},{4,8},{8,12},{12,16},{16,20},{20,24},{24,28},{28,0},{1,5},{5... | collective-permute-start | bytes 13074440 | tf_op jit(solution)/shard_map/ppermute | solution.py:21
  771.5 4.5 collective-permute-start.7
  791.3 286.7 %all-gather.11.cloned.1.call-start = ((), (), s32[]{:S(2)}) async-start(), calls=%async_computation.3 | async-start | bytes 18874368 | tf_op jit(solution)/shard_map/all_gather | solution.py:100
  792.1 380.9 %all-gather.17.cloned.1.call-start = ((), (), s32[]{:S(2)}) async-start(), calls=%async_computation.8 | async-start | bytes 10485760 | tf_op jit(solution)/shard_map/all_gather | solution.py:41
  1116.3 603.5 %reduce-scatter.8.cloned.1.call-start = ((), (), s32[]{:S(2)}) async-start(), calls=%async_computation.6 | async-start | bytes 37748736 | tf_op jit(solution)/shard_map/reduce_scatter | solution.py:284
  1134.2 1688.3 %reduce-scatter.6.cloned.1.call-start = ((), (), s32[]{:S(2)}) async-start(), calls=%async_computation.5 | async-start | bytes 78446592 | tf_op jit(solution)/shard_map/reduce_scatter | solution.py:280
  1231.6 3.2 collective-permute-start.8
  1262.1 1632.5 %reduce-scatter.10.cloned.1.call-start = ((), (), s32[]{:S(2)}) async-start(), calls=%async_computation.9 | async-start | bytes 2506752
  1264.6 2294.3 %all-gather.13.cloned.1.call-start = ((), (), s32[]{:S(2)}) async-start(), calls=%async_computation.4 | async-start | bytes 39223296 | tf_op jit(solution)/shard_map/all_gather | solution.py:173
  1265.3 2523.3 %all-reduce.20.cloned.1.call-start = ((), (), s32[]{:S(2)}) async-start(), calls=%async_computation.10 | async-start | bytes 25821184 | tf_op jit(solution)/shard_map/psum | solution.py:286
  2895.7 682.1 %copy-start.39 = (f32[4096]{0:T(1024)S(1)}, f32[4096]{0:T(1024)}, u32[]{:S(2)}) copy-start(f32[4096]{0:T(1024)} %get-tuple-element.254) | copy-start | bytes 49156
  2895.7 729.4 %copy-start.41 = (f32[256]{0:T(256)S(1)}, f32[256]{0:T(256)}, u32[]{:S(2)}) copy-start(f32[256]{0:T(256)} %copy-done.40) | copy-start | bytes 3076
  (54 other events, 1085.1 us)
Sparse Core Ops, SparseCore 0:
  791.4 56.7 all-gather.14
  850.4 227.6 all-gather.10
  1116.4 56.4 all-gather.16
  1176.5 543.1 reduce-scatter.7
  1723.5 1098.9 reduce-scatter.5
  2826.8 67.7 reduce-scatter.9
  2896.1 662.7 all-gather.12
  3561.7 226.8 all-reduce.19
